TPU v7x, 32 devices: a whole 2x2x4 slice. The times are simulated.
32 devices in a mesh: tm: 2 (over x), row: 4 (over y, core), col: 4 (over z).
Axes of the slice: x: 2, y: 2, z: 4, core: 2. Of those that a mesh axis runs over, the one named last changes fastest.
Arguments:
- returns: bfloat16 [1440, 4096], P('tm', ('row', 'col')), may hold values from -50 to 50
- block_bars: int32 [8], replicated, may hold values from 90 to 180
Outputs:
- correlation: bfloat16 [8, 4096, 4096], P('tm', 'row', 'col')
All inputs are finite; a program needn't handle non-finite values.
Results may differ from a plain program's by a relative error of at most 0.0034.
Values may be sent and summed in bfloat16 or wider, within the bound.
A program may use at most 128 MiB of HBM per device.

v0:
```python
import jax
import jax.numpy as jnp
from jax import lax
from jax.sharding import PartitionSpec as P

BLK = 180


def shifted(block, axis, distance):
    devices = range(lax.axis_size(axis))
    route = [(i - distance, i) for i in devices if i - distance in devices]
    return lax.ppermute(block, axis, route)


def center(raw, counts):
    nblocks = raw.shape[0] // BLK
    values = raw.reshape(nblocks, BLK, raw.shape[1]).astype(jnp.float32)
    mask = (lax.broadcasted_iota(jnp.int32, (nblocks, BLK, 1), 1) < counts[:, None, None]).astype(
        jnp.float32
    )
    divisor = jnp.maximum(counts, 1).astype(jnp.float32)
    means = jnp.sum(mask * values, axis=1) / divisor[:, None]
    centered = (mask * (values - means[:, None, :])).astype(jnp.bfloat16)
    return (centered, means)


def spread_tiles(raw, counts):
    whole = lax.all_gather(raw, ("row", "col"), axis=1, tiled=True)
    centered, means = center(whole, counts)
    width = centered.shape[2]
    row_width = width // lax.axis_size("row")
    col_width = width // lax.axis_size("col")
    row_start = lax.axis_index("row") * row_width
    col_start = lax.axis_index("col") * col_width
    row_cent = lax.dynamic_slice_in_dim(centered, row_start, row_width, 2)
    col_cent = lax.dynamic_slice_in_dim(centered, col_start, col_width, 2)
    row_mean = lax.dynamic_slice_in_dim(means, row_start, row_width, 1)
    col_mean = lax.dynamic_slice_in_dim(means, col_start, col_width, 1)
    return (row_cent, col_cent, row_mean, col_mean)


def squares(row_cent, col_cent):
    row_f = row_cent.astype(jnp.float32)
    col_f = col_cent.astype(jnp.float32)
    return (jnp.sum(row_f * row_f, axis=1), jnp.sum(col_f * col_f, axis=1))


def statistics(row_cent, col_cent, row_mean, col_mean):
    gram = jnp.einsum("kti,ktj->kij", row_cent, col_cent, preferred_element_type=jnp.float32)
    row_var, col_var = squares(row_cent, col_cent)
    return (gram, row_mean, col_mean, row_var, col_var)


def on_device(returns, block_bars):
    nbars = returns.shape[0]
    nblocks = nbars // BLK
    tm_index = lax.axis_index("tm")
    counts = lax.dynamic_slice_in_dim(block_bars, tm_index * nblocks, nblocks)
    before = lax.dynamic_slice_in_dim(block_bars, jnp.maximum(tm_index * nblocks - 1, 0), 1)
    prev_count = jnp.where(tm_index > 0, before, jnp.zeros_like(before))
    earlier = shifted(returns[nbars - BLK :], "tm", 1)
    pieces = spread_tiles(
        jnp.concatenate([earlier, returns], axis=0), jnp.concatenate([prev_count, counts], axis=0)
    )
    gram, row_mean, col_mean, row_var, col_var = statistics(*pieces)
    gram_pair = gram[:-1] + gram[1:]
    rvar_pair = row_var[:-1] + row_var[1:]
    cvar_pair = col_var[:-1] + col_var[1:]
    rmean_a, cmean_a = (row_mean[:-1], col_mean[:-1])
    rmean_b, cmean_b = (row_mean[1:], col_mean[1:])
    count_a = jnp.concatenate([prev_count, counts[:-1]], axis=0).astype(jnp.float32)
    count_b = counts.astype(jnp.float32)
    weight = count_a * count_b / (count_a + count_b)
    row_delta = rmean_a - rmean_b
    col_delta = cmean_a - cmean_b
    cov = gram_pair + weight[:, None, None] * row_delta[:, :, None] * col_delta[:, None, :]
    row_total = rvar_pair + weight[:, None] * row_delta * row_delta
    col_total = cvar_pair + weight[:, None] * col_delta * col_delta
    row_inv = lax.rsqrt(row_total)
    col_inv = lax.rsqrt(col_total)
    return (cov * row_inv[:, :, None] * col_inv[:, None, :]).astype(jnp.bfloat16)


def solution(mesh):
    placed = (P("tm", ("row", "col")), P())
    return jax.shard_map(
        on_device, mesh=mesh, in_specs=placed, out_specs=P("tm", "row", "col"), check_vma=False
    )
```

profile of v0, /device:TPU:6, one launch (start us, length us, event | category | flops | bytes accessed | tf_op | source)
XLA Modules:
  0.0 141.2 jit_solution(5978978311850477699)
XLA Ops:
  6.5 0.0 all-gather.2.cloned.1.call-start
  6.5 0.9 slice.36
  7.5 1.3 collective-permute-start
  8.8 5.2 %collective-permute-done = bf16[180,256]{1,0:T(8,128)(2,1)S(1)} collective-permute-done((bf16[180,256]{1,0:T(8,128)(2,1)S(1)}, bf16[180,256]{1,0:T(8,128)(2,1)S(1)}, u32[]{:S(2)}, u32[]{:S(2)}) %collective-permute-start) | collective-permute-done | bytes 92192 | tf_op jit(solution)/shard_map/ppermute | solution.py:12
  13.9 1.8 %pad_maximum_fusion = bf16[900,256]{1,0:T(8,128)(2,1)} fusion(bf16[720,256]{1,0:T(8,128)(2,1)} %param.2, bf16[180,256]{1,0:T(8,128)(2,1)S(1)} %collective-permute-done), kind=kLoop, calls=%fused_computation.12 | loop fusion | flops 921600 | bytes 921600 | tf_op jit(solution)/shard_map/concatenate | solution.py:63
  15.8 0.0 all-gather.2.cloned.1.call-update
  15.8 1.2 dynamic_slice.18
  17.0 0.7 dynamic_slice.19
  18.3 0.7 add_divide_fusion
  19.1 0.1 maximum_convert_fusion
  19.2 0.1 fusion.11
  19.2 69.7 %all-gather.2.cloned.1.call-done = bf16[900,4096]{1,0:T(8,128)(2,1)} async-done(((bf16[900,256]{1,0:T(8,128)(2,1)}), bf16[900,4096]{1,0:T(8,128)(2,1)}) %all-gather.2.cloned.1.call-update) | async-done | bytes 7372816 | tf_op jit(solution)/shard_map/all_gather | solution.py:28
  89.0 13.3 %reshape.67 = f32[5,180,4096]{2,1,0:T(8,128)} reshape(bf16[900,4096]{1,0:T(8,128)(2,1)} %all-gather.2.cloned.1.call-done) | data formatting | bytes 22118400 | tf_op jit(solution)/shard_map/convert_element_type | solution.py:17
  102.2 7.5 %multiply_reduce_fusion = f32[5,4096]{1,0:T(8,128)S(1)} fusion(f32[5,180,4096]{2,1,0:T(8,128)} %reshape.67, f32[5,180]{1,0:T(8,128)S(1)} %fusion.11), kind=kLoop, calls=%fused_computation.6 | loop fusion | flops 7352320 | bytes 14831120 | tf_op jit(solution)/shard_map/reduce_sum | solution.py:22
  109.8 0.1 broadcast_divide_fusion
  109.8 11.1 %multiply_convert_fusion = bf16[5,180,4096]{2,1,0:T(8,128)(2,1)} fusion(f32[5,180,4096]{2,1,0:T(8,128)} %reshape.67, f32[5,4096]{1,0:T(8,128)S(1)} %broadcast_divide_fusion, f32[5,180]{1,0:T(8,128)S(1)} %fusion.11), kind=kLoop, calls=%fused_computation.5 | loop fusion | flops 11059200 | bytes 22203920 | tf_op jit(solution)/shard_map/convert_element_type | solution.py:23
  121.0 3.0 %multiply_reduce_fusion.2 = (f32[5,1024]{1,0:T(8,128)S(1)}, f32[5,1024]{1,0:T(8,128)S(1)}) fusion(bf16[5,180,4096]{2,1,0:T(8,128)(2,1)} %multiply_convert_fusion, s32[]{:T(128)S(6)} %select_n.23, s32[]{:T(128)S(6)} %select_n.24), kind=kLoop, calls=%fused_computation.8 | loop fusion | flops 5519360 | bytes 3727368 | tf_op jit(solution)/shard_map/reduce_sum | solution.py:45
  124.0 5.1 %fusion.4 = f32[5,1024,1024]{2,1,0:T(8,128)S(1)} fusion(bf16[5,180,4096]{2,1,0:T(8,128)(2,1)} %multiply_convert_fusion, s32[]{:T(128)S(6)} %select_n.24, s32[]{:T(128)S(6)} %select_n.23), kind=kOutput, calls=%fused_computation.9 | convolution fusion | flops 1887436800 | bytes 24739848 | tf_op jit(solution)/shard_map/kti,ktj->kij/dot_general | solution.py:49
  129.0 0.1 fusion.10
  129.2 5.2 %fusion.3 = bf16[4,1024,1024]{2,1,0:T(8,128)(2,1)} fusion(f32[5,1024,1024]{2,1,0:T(8,128)S(1)} %fusion.4, f32[4,1024]{1,0:T(4,128)S(1)} %get-tuple-element.13, f32[4,1024]{1,0:T(4,128)S(1)} %get-tuple-element.7, f32[4,1024]{1,0:T(4,128)S(1)} %get-tuple-element.14, f32[4,1024]{1,0:T(4,128)S(1)} %get-tuple-element.8), kind=kLoop, calls=%fused_computation.4 | loop fusion | flops 25165824 | bytes 42008576 | tf_op jit(solution)/shard_map/convert_element_type | solution.py:81
Async XLA Ops:
  6.5 82.4 %all-gather.2.cloned.1.call-start = ((), (), s32[]{:S(2)}) async-start(), calls=%async_computation | async-start | bytes 7868416 | tf_op jit(solution)/shard_map/all_gather | solution.py:28
  7.5 6.5 %collective-permute-start = (bf16[180,256]{1,0:T(8,128)(2,1)S(1)}, bf16[180,256]{1,0:T(8,128)(2,1)S(1)}, u32[]{:S(2)}, u32[]{:S(2)}) collective-permute-start(bf16[180,256]{1,0:T(8,128)(2,1)S(1)} %slice.36), channel_id=1, source_target_pairs={{0,16},{1,17},{2,18},{3,19},{4,20},{5,21},{6,22},{7,23},{8,24},{9,... | collective-permute-start | bytes 276488 | tf_op jit(solution)/shard_map/ppermute | solution.py:12
Sparse Core Ops, SparseCore 0:
  15.9 73.0 all-gather.1
where the time goes:
time: 143 us; the launch traced here: 141 us
  waiting for transfers between devices  74.9 us (52%)
  other arithmetic  29.7 us (21%)
  local copies, waits for them, and re-layouts  16.1 us (11%)
  between operations  14 us (10%)
  matrix products  5.08 us (4%)
    all_gather x1, waiting for transfers between devices, spread_tiles(): whole = lax.all_gather(raw, ('row', 'col'), axis=1, tiled=True)  69.7 us
    convert_element_type x1, local copies, waits for them, and re-layouts, center(): values = raw.reshape(nblocks, BLK, raw.shape[1]).astype(jnp.float32)  13.3 us
    convert_element_type x1, other arithmetic, center(): centered = (mask * (values - means[:, None, :])).astype(jnp.bfloat16)  11.1 us
    reduce_sum x1, other arithmetic, center(): means = jnp.sum(mask * values, axis=1) / divisor[:, None]  7.51 us
    convert_element_type x1, other arithmetic, on_device(): (cov * row_inv[:, :, None] * col_inv[:, None, :]).astype(jnp.bfloat16)  5.18 us
    ppermute x1, waiting for transfers between devices, shifted(): return lax.ppermute(block, axis, route)  5.17 us
    dot_general x1, matrix products, statistics(): jnp.einsum('kti,ktj->kij', row_cent, col_cent, preferred_element_type=jnp...  5.08 us
    reduce_sum x1, other arithmetic, squares(): return (jnp.sum(row_f * row_f, axis=1), jnp.sum(col_f * col_f, axis=1))  3 us
  transfers between devices with their start and end apart: 2, of which 2 were waited for; matrix products, arithmetic and copies ran while one was open for 2% of the time, Pallas kernels for 0%

commit v1 on v0

v1 whole, which is shorter than its diff:
```python
import functools

import jax
import jax.numpy as jnp
from jax import lax
from jax.experimental import pallas as pl
from jax.experimental.pallas import tpu as pltpu
from jax.sharding import PartitionSpec as P

TILE = 16
DEPTH = 256
MESH = pl.DeviceIdType.MESH


def up(value, step=TILE):
    return -(-value // step) * step


def down(value, step=TILE):
    return value // step * step


def kernel(
    sizes, nb, blk, bars_ref, x_ref, out_ref,
    raw, lhs, rhs, stats, own_sem, row_send, row_recv, next_send, hub_send, col_recv, relay_send,
):
    T, R, C = sizes
    nbars, width = x_ref.shape
    t, r, c = lax.axis_index("tm"), lax.axis_index("row"), lax.axis_index("col")
    hub = r == c
    last = nb - 1
    cuts = [up(blk * b) for b in range(nb - 1)] + [down(blk * last), nbars]
    spans = [(cuts[b], cuts[b + 1] - cuts[b]) for b in range(nb)]
    spans.append((nbars, nbars - cuts[last]))
    before = nb

    def rows(ch):
        return pl.ds(*spans[ch])

    barrier = pltpu.get_barrier_semaphore()

    def greet(where):
        pl.semaphore_signal(barrier, inc=1, device_id=where, device_id_type=MESH)

    ends = ((c > 0, {"col": c - 1}), (c < C - 1, {"col": c + 1}), (t > 0, {"tm": t - 1}), (t < T - 1, {"tm": t + 1}))
    expected = R - 1
    for there, where in ends:
        pl.when(there)(functools.partial(greet, where))
        expected = expected + there.astype(jnp.int32)
    for step in range(1, R):
        greet({"row": lax.rem(r + step, R)})
    pl.semaphore_wait(barrier, expected)

    def remote(src, dst, send, recv, where):
        return pltpu.make_async_remote_copy(
            src_ref=src, dst_ref=dst, send_sem=send, recv_sem=recv, device_id=where, device_id_type=MESH
        )

    sent = []

    def start(there, make):
        @pl.when(there)
        def _():
            make().start()

        sent.append((there, make))

    def row_copy(ch, k, to_right, src):
        where = {"col": c + 1 if to_right else c - 1}
        return remote(src, raw.at[0, k, rows(ch)], row_send.at[ch, k, int(to_right)], row_recv.at[ch, k], where)

    def own_send(ch):
        src = x_ref.at[rows(ch)]
        start(c < C - 1, lambda: row_copy(ch, c, True, src))
        start(c > 0, lambda: row_copy(ch, c, False, src))

    def spread(there, ch, k, src):
        at_hub = jnp.logical_and(there, hub)
        chips = R // 2
        chip = r // 2
        for step in range(1, chips):
            where = {"row": 2 * lax.rem(chip + step, chips) + lax.rem(k, 2)}
            start(at_hub, lambda where=where, step=step: remote(
                src, raw.at[1, k, rows(ch)], hub_send.at[ch, k, step], col_recv.at[ch, k], where))
        partner = {"row": r + 1 - 2 * lax.rem(r, 2)}
        start(at_hub, lambda: remote(src, raw.at[1, k, rows(ch)], hub_send.at[ch, k, 0], col_recv.at[ch, k], partner))
        if ch == last:
            start(jnp.logical_and(there, t < T - 1), lambda: remote(
                src, raw.at[0, k, rows(before)], next_send.at[k], row_recv.at[before, k], {"tm": t + 1}))

    def row_arrive(there, ch, k):
        @pl.when(there)
        def _():
            piece = raw.at[0, k, rows(ch)]
            remote(piece, piece, next_send.at[k], row_recv.at[ch, k], {"row": r}).wait_recv()

    def row_phase(ch):
        for d in range(1, C):
            for from_left in (True, False):
                k0 = c - d if from_left else c + d
                there = k0 >= 0 if from_left else k0 < C
                k = jnp.clip(k0, 0, C - 1)
                row_arrive(there, ch, k)
                src = raw.at[0, k, rows(ch)]
                on = c < C - 1 if from_left else c > 0
                start(jnp.logical_and(there, on), lambda k=k, src=src, right=from_left: row_copy(ch, k, right, src))
                spread(there, ch, k, src)

    def before_phase():
        for k in range(C):
            row_arrive(t > 0, before, k)
            spread(t > 0, before, jnp.int32(k), raw.at[0, k, rows(before)])

    def col_phase(ch, there):
        relay = jnp.logical_and(there, r // 2 != c // 2)
        partner = {"row": r + 1 - 2 * lax.rem(r, 2)}
        for k in range(C):
            piece = raw.at[1, k, rows(ch)]

            @pl.when(jnp.logical_and(there, jnp.logical_not(hub)))
            def _():
                remote(piece, piece, next_send.at[k], col_recv.at[ch, k], {"row": r}).wait_recv()

            start(jnp.logical_and(relay, lax.rem(r, 2) == k % 2), lambda piece=piece, k=k: remote(
                piece, piece, relay_send.at[ch, k], col_recv.at[ch, k], partner))

    base = t * nb

    def count(j):
        if j:
            return bars_ref[base + j - 1]
        return jnp.where(t > 0, bars_ref[jnp.maximum(base - 1, 0)], 0)

    def center(j):
        b = j - 1 if j else last
        low = down(blk * b)
        depth = up(blk * (b + 1)) - low
        offset = blk * b - low
        first = low if j else spans[before][0]
        n = count(j)
        bar = lax.broadcasted_iota(jnp.int32, (depth, width), 0) - offset
        mask = jnp.logical_and(bar >= 0, bar < n)
        divisor = jnp.full((1, width), jnp.maximum(n, 1).astype(jnp.float32))
        for side in range(2):
            source = 0 if side == 0 else jnp.where(hub, 0, 1)

            def piece(k, carry):
                values = raw[source, k, pl.ds(first, depth), :].astype(jnp.float32)
                mean = jnp.sum(jnp.where(mask, values, 0.0), axis=0, keepdims=True) / divisor
                cent = jnp.where(mask, values - mean, 0.0).astype(jnp.bfloat16)
                wide = cent.astype(jnp.float32)
                stats[side, k, 2 * j : 2 * j + 1, :] = mean
                stats[side, k, 2 * j + 1 : 2 * j + 2, :] = jnp.sum(wide * wide, axis=0, keepdims=True)
                if depth < DEPTH:
                    wide = jnp.concatenate([wide, jnp.zeros((DEPTH - depth, width), jnp.float32)], axis=0)
                at = pl.ds(pl.multiple_of(k * width, width), width)
                if side == 0:
                    lhs[at, j * DEPTH : (j + 1) * DEPTH] = wide.T.astype(jnp.bfloat16)
                else:
                    rhs[j * DEPTH : (j + 1) * DEPTH, at] = wide.astype(jnp.bfloat16)
                return carry

            lax.fori_loop(0, C, piece, 0)

    def emit(b):
        def pair(side, k):
            mean_a, var_a = stats[side, k, 2 * b : 2 * b + 1, :], stats[side, k, 2 * b + 1 : 2 * b + 2, :]
            mean_b, var_b = stats[side, k, 2 * b + 2 : 2 * b + 3, :], stats[side, k, 2 * b + 3 : 2 * b + 4, :]
            delta = mean_a - mean_b
            return weight, delta, lax.rsqrt(var_a + var_b + weight * delta * delta)

        count_a = jnp.full((1, width), count(b).astype(jnp.float32))
        count_b = jnp.full((1, width), count(b + 1).astype(jnp.float32))
        weight = count_a * count_b / (count_a + count_b)
        cols = [pair(1, k)[1:] for k in range(C)]

        def tile(k, carry):
            w, delta, inv = pair(0, k)
            both = jnp.concatenate([w * delta, inv, jnp.zeros((6, width), jnp.float32)], axis=0).T
            scaled, inv_i = both[:, 0:1], both[:, 1:2]
            at = pl.ds(pl.multiple_of(k * width, width), width)
            a = lhs[at, b * DEPTH : (b + 2) * DEPTH]
            for m in range(C):
                span = slice(m * width, (m + 1) * width)
                gram = jnp.dot(a, rhs[b * DEPTH : (b + 2) * DEPTH, span], preferred_element_type=jnp.float32)
                cov = gram + scaled * cols[m][0]
                out_ref[b, at, span] = (cov * inv_i * cols[m][1]).astype(jnp.bfloat16)
            return carry

        lax.fori_loop(0, C, tile, 0)

    order = [last] + list(range(last))
    true = t >= 0
    mine = pltpu.make_async_copy(x_ref, raw.at[0, c, pl.ds(0, nbars)], own_sem)
    own_send(order[0])
    spread(true, order[0], c, x_ref.at[rows(order[0])])
    own_send(order[1])
    spread(true, order[1], c, x_ref.at[rows(order[1])])
    mine.start()

    @pl.when(t == 0)
    def _():
        low, depth = spans[before]
        for side in range(2):
            for k in range(C):
                raw[side, k, pl.ds(low, depth), :] = jnp.zeros((depth, width), jnp.bfloat16)

    for i, ch in enumerate(order):
        row_phase(ch)
        if i + 2 < nb:
            own_send(order[i + 2])
            spread(true, order[i + 2], c, x_ref.at[rows(order[i + 2])])
        if i >= 1:
            col_phase(order[i - 1], true)
        if i == 0:
            mine.wait()
        if i == 2:
            before_phase()
            center(last + 1)
            center(1)
        if i == nb - 1:
            col_phase(before, t > 0)
            center(0)
            emit(0)
            center(2)
            emit(1)
    col_phase(order[-1], true)
    for b in range(2, last):
        center(b + 1)
    for b in range(2, nb):
        emit(b)
    for there, make in sent:

        @pl.when(there)
        def _():
            make().wait_send()


def on_device(sizes, returns, block_bars):
    T, R, C = sizes
    nbars, width = returns.shape
    nb = block_bars.shape[0] // T
    blk = nbars // nb
    tail = nbars - down(blk * (nb - 1))
    dma = pltpu.SemaphoreType.DMA
    return pl.pallas_call(
        functools.partial(kernel, sizes, nb, blk),
        out_shape=jax.ShapeDtypeStruct((nb, C * width, R * width), jnp.bfloat16),
        in_specs=[pl.BlockSpec(memory_space=pltpu.SMEM), pl.BlockSpec(memory_space=pl.ANY)],
        out_specs=pl.BlockSpec(memory_space=pltpu.VMEM),
        scratch_shapes=[
            pltpu.VMEM((2, C, nbars + tail, width), jnp.bfloat16),
            pltpu.VMEM((C * width, (nb + 1) * DEPTH), jnp.bfloat16),
            pltpu.VMEM(((nb + 1) * DEPTH, R * width), jnp.bfloat16),
            pltpu.VMEM((2, C, up(2 * (nb + 1)), width), jnp.float32),
            dma,
            dma((nb, C, 2)),
            dma((nb + 1, C)),
            dma((C,)),
            dma((nb + 1, C, R // 2)),
            dma((nb + 1, C)),
            dma((nb + 1, C)),
        ],
        compiler_params=pltpu.CompilerParams(
            collective_id=0, has_side_effects=True, vmem_limit_bytes=48 * 1024 * 1024
        ),
        name="gather_correlate",
    )(block_bars, returns)


def solution(mesh):
    sizes = (mesh.shape["tm"], mesh.shape["row"], mesh.shape["col"])
    placed = (P("tm", ("row", "col")), P())
    return jax.shard_map(
        functools.partial(on_device, sizes),
        mesh=mesh, in_specs=placed, out_specs=P("tm", "row", "col"), check_vma=False,
    )
```

time: 143 us -> 70.6 us (0.49); the launches traced: 141 us -> 70.4 us
  waiting for transfers between devices: 74.9 us -> 0 us
  Pallas kernels: 0 us -> 61 us
  other arithmetic: 29.7 us -> 0 us
  between operations: 14 us -> 0.01 us
  local copies, waits for them, and re-layouts: 16.1 us -> 9.4 us
  matrix products: 5.08 us -> 0 us
    all_gather x1 -> x0, waiting for transfers between devices: 69.7 us -> none  [spread_tiles(): whole = lax.all_gather(raw, ('row', 'col'), axis=1, tiled=True)]
    pallas_call x0 -> x1, Pallas kernels: none -> 61 us  [on_device(): pl.pallas_call(functools.partial(kernel, sizes, nb, blk), out_shape=jax.S...]
    convert_element_type x4 -> x0, other arithmetic: 16.4 us -> none  [the longest x1 11.1 us: center(): centered = (mask * (values - means[:, None, :])).astype(jnp.bfloat16)]
    convert_element_type x1 -> x0, local copies, waits for them, and re-layouts: 13.3 us -> none  [center(): values = raw.reshape(nblocks, BLK, raw.shape[1]).astype(jnp.float32)]
    reduce_sum x2 -> x0, other arithmetic: 10.5 us -> none  [the longest x1 7.51 us: center(): means = jnp.sum(mask * values, axis=1) / divisor[:, None]]
    unnamed x0 -> x5, local copies, waits for them, and re-layouts: none -> 9.4 us
    ppermute x1 -> x0, waiting for transfers between devices: 5.17 us -> none  [shifted(): return lax.ppermute(block, axis, route)]
    dot_general x1 -> x0, matrix products: 5.08 us -> none  [statistics(): jnp.einsum('kti,ktj->kij', row_cent, col_cent, preferred_element_type=jnp...]
  transfers between devices with their start and end apart: 2 -> 0, of which waited for: 2 -> 0; matrix products, arithmetic and copies ran while one was open for 2% -> 0% of each run, Pallas kernels for 0% -> 0%
where the time goes in v1:
time: 70.6 us; the launch traced here: 70.4 us
  Pallas kernels  61 us (86%)
  local copies, waits for them, and re-layouts  9.4 us (13%)
    pallas_call x1, Pallas kernels, on_device(): pl.pallas_call(functools.partial(kernel, sizes, nb, blk), out_shape=jax.S...  61 us
    unnamed x5, local copies, waits for them, and re-layouts  9.4 us

profile of v1, /device:TPU:6, one launch (start us, length us, event | category | flops | bytes accessed | tf_op | source)
XLA Modules:
  0.0 70.4 jit_solution(3722373335317148420)
XLA Ops:
  0.0 0.0 copy-start
  0.0 1.0 %copy-done = bf16[720,256]{1,0:T(8,128)(2,1)S(1)} copy-done((bf16[720,256]{1,0:T(8,128)(2,1)S(1)}, bf16[720,256]{1,0:T(8,128)(2,1)}, u32[]{:S(2)}) %copy-start) | copy-done | bytes 368664
  1.0 0.0 copy-start.1
  1.0 0.7 copy-done.1
  1.6 61.0 %gather_correlate.1 = bf16[4,1024,1024]{2,1,0:T(8,128)(2,1)} custom-call(s32[8]{0:T(128)S(1)} %copy-done.1, bf16[720,256]{1,0:T(8,128)(2,1)S(1)} %copy-done), custom_call_target="tpu_custom_call" | custom-call | tf_op jit(solution)/shard_map/gather_correlate/pallas_call | solution.py:246
  62.6 7.8 %copy.4 = bf16[4,1024,1024]{2,1,0:T(8,128)(2,1)} copy(bf16[4,1024,1024]{2,1,0:T(8,128)(2,1)} %gather_correlate.1) | data formatting | bytes 16777216
Async XLA Ops:
  0.0 1.0 %copy-start = (bf16[720,256]{1,0:T(8,128)(2,1)S(1)}, bf16[720,256]{1,0:T(8,128)(2,1)}, u32[]{:S(2)}) copy-start(bf16[720,256]{1,0:T(8,128)(2,1)} %x_ref.1) | copy-start | bytes 1105924
  1.0 0.7 copy-start.1

commit v2 on v1

--- a/solution.py
+++ b/solution.py
@@ -245,7 +245,7 @@
     dma = pltpu.SemaphoreType.DMA
     return pl.pallas_call(
         functools.partial(kernel, sizes, nb, blk),
-        out_shape=jax.ShapeDtypeStruct((nb, C * width, R * width), jnp.bfloat16),
+        out_shape=pltpu.VMEM((nb, C * width, R * width), jnp.bfloat16),
         in_specs=[pl.BlockSpec(memory_space=pltpu.SMEM), pl.BlockSpec(memory_space=pl.ANY)],
         out_specs=pl.BlockSpec(memory_space=pltpu.VMEM),
         scratch_shapes=[
@@ -262,7 +262,7 @@
             dma((nb + 1, C)),
         ],
         compiler_params=pltpu.CompilerParams(
-            collective_id=0, has_side_effects=True, vmem_limit_bytes=48 * 1024 * 1024
+            collective_id=0, has_side_effects=True, vmem_limit_bytes=32 * 1024 * 1024
         ),
         name="gather_correlate",
     )(block_bars, returns)

time: 70.6 us -> 63 us (0.89)
  local copies, waits for them, and re-layouts: 9.4 us -> 5.04 us
  Pallas kernels: 61 us -> 57.8 us
    unnamed x5, local copies, waits for them, and re-layouts: 9.4 us -> 5.04 us
    pallas_call x1, Pallas kernels: 61 us -> 57.8 us  [on_device(): pl.pallas_call(functools.partial(kernel, sizes, nb, blk), out_shape=pltpu...]
where the time goes in v2:
time: 63 us; the launch traced here: 62.8 us
  Pallas kernels  57.8 us (92%)
  local copies, waits for them, and re-layouts  5.04 us (8%)
    pallas_call x1, Pallas kernels, on_device(): pl.pallas_call(functools.partial(kernel, sizes, nb, blk), out_shape=pltpu...  57.8 us
    unnamed x5, local copies, waits for them, and re-layouts  5.04 us

profile of v2, /device:TPU:6, one launch (start us, length us, event | category | flops | bytes accessed | tf_op | source)
XLA Modules:
  0.0 62.8 jit_solution(9639250318512046446)
XLA Ops:
  0.0 0.0 copy-start
  0.0 1.0 %copy-done = bf16[720,256]{1,0:T(8,128)(2,1)S(1)} copy-done((bf16[720,256]{1,0:T(8,128)(2,1)S(1)}, bf16[720,256]{1,0:T(8,128)(2,1)}, u32[]{:S(2)}) %copy-start) | copy-done | bytes 368664
  1.0 0.0 copy-start.1
  1.0 0.7 %copy-done.1 = s32[8]{0:T(128)S(1)} copy-done((s32[8]{0:T(128)S(1)}, s32[8]{0:T(128)}, u32[]{:S(2)}) %copy-start.1) | copy-done | bytes 56
  1.6 57.8 %gather_correlate.1 = bf16[4,1024,1024]{2,1,0:T(8,128)(2,1)S(1)} custom-call(s32[8]{0:T(128)S(1)} %copy-done.1, bf16[720,256]{1,0:T(8,128)(2,1)S(1)} %copy-done), custom_call_target="tpu_custom_call" | custom-call | tf_op jit(solution)/shard_map/gather_correlate/pallas_call | solution.py:246
  59.4 3.4 %copy.4 = bf16[4,1024,1024]{2,1,0:T(8,128)(2,1)} copy(bf16[4,1024,1024]{2,1,0:T(8,128)(2,1)S(1)} %gather_correlate.1) | data formatting | bytes 16777216
Async XLA Ops:
  0.0 1.0 %copy-start = (bf16[720,256]{1,0:T(8,128)(2,1)S(1)}, bf16[720,256]{1,0:T(8,128)(2,1)}, u32[]{:S(2)}) copy-start(bf16[720,256]{1,0:T(8,128)(2,1)} %x_ref.1) | copy-start | bytes 1105924
  1.0 0.7 %copy-start.1 = (s32[8]{0:T(128)S(1)}, s32[8]{0:T(128)}, u32[]{:S(2)}) copy-start(s32[8]{0:T(128)} %bars_ref.1) | copy-start | bytes 100

commit v3 on v2

v3 whole, which is shorter than its diff:
```python
import functools

import jax
import jax.numpy as jnp
from jax import lax
from jax.experimental import pallas as pl
from jax.experimental.pallas import tpu as pltpu
from jax.sharding import PartitionSpec as P

TILE = 16
DEPTH = 256
LAG = 4
MESH = pl.DeviceIdType.MESH


def up(value, step=TILE):
    return -(-value // step) * step


def down(value, step=TILE):
    return value // step * step


def kernel(
    sizes, nb, blk, bars_in, x_ref, out_ref,
    bars_ref, raw, lhs, rhs, stats, kept, final, own_sem, bars_sem, row_send, row_recv, next_send, hub_send, col_recv, relay_send,
):
    T, R, C = sizes
    nbars, width = x_ref.shape
    t, r, c = lax.axis_index("tm"), lax.axis_index("row"), lax.axis_index("col")
    hub = r == c
    last = nb - 1
    cuts = [up(blk * b) for b in range(nb - 1)] + [down(blk * last), nbars]
    spans = [(cuts[b], cuts[b + 1] - cuts[b]) for b in range(nb)]
    spans.append((nbars, nbars - cuts[last]))
    before = nb

    def rows(ch):
        return pl.ds(*spans[ch])

    barrier = pltpu.get_barrier_semaphore()

    def greet(where):
        pl.semaphore_signal(barrier, inc=1, device_id=where, device_id_type=MESH)

    ends = ((c > 0, {"col": c - 1}), (c < C - 1, {"col": c + 1}), (t > 0, {"tm": t - 1}), (t < T - 1, {"tm": t + 1}))
    expected = R - 1
    for there, where in ends:
        pl.when(there)(functools.partial(greet, where))
        expected = expected + there.astype(jnp.int32)
    for step in range(1, R):
        greet({"row": lax.rem(r + step, R)})
    pl.semaphore_wait(barrier, expected)

    def remote(src, dst, send, recv, where):
        return pltpu.make_async_remote_copy(
            src_ref=src, dst_ref=dst, send_sem=send, recv_sem=recv, device_id=where, device_id_type=MESH
        )

    sent = []

    def start(there, make):
        @pl.when(there)
        def _():
            make().start()

        sent.append((there, make))

    def row_copy(ch, k, to_right, src):
        where = {"col": c + 1 if to_right else c - 1}
        return remote(src, raw.at[0, k, rows(ch)], row_send.at[ch, k, int(to_right)], row_recv.at[ch, k], where)

    def own_send(ch):
        src = x_ref.at[rows(ch)]
        start(c < C - 1, lambda: row_copy(ch, c, True, src))
        start(c > 0, lambda: row_copy(ch, c, False, src))

    def spread(there, ch, k, src):
        at_hub = jnp.logical_and(there, hub)
        chips = R // 2
        chip = r // 2
        for step in range(1, chips):
            where = {"row": 2 * lax.rem(chip + step, chips) + lax.rem(k, 2)}
            start(at_hub, lambda where=where, step=step: remote(
                src, raw.at[1, k, rows(ch)], hub_send.at[ch, k, step], col_recv.at[ch, k], where))
        partner = {"row": r + 1 - 2 * lax.rem(r, 2)}
        start(at_hub, lambda: remote(src, raw.at[1, k, rows(ch)], hub_send.at[ch, k, 0], col_recv.at[ch, k], partner))
        if ch == last:
            start(jnp.logical_and(there, t < T - 1), lambda: remote(
                src, raw.at[0, k, rows(before)], next_send.at[k], row_recv.at[before, k], {"tm": t + 1}))

    def row_arrive(there, ch, k):
        @pl.when(there)
        def _():
            piece = raw.at[0, k, rows(ch)]
            remote(piece, piece, next_send.at[k], row_recv.at[ch, k], {"row": r}).wait_recv()

    def row_event(ch, k, there, on, to_right):
        if to_right is None and ch != before:
            return
        row_arrive(there, ch, k)
        src = raw.at[0, k, rows(ch)]
        if ch != before:
            start(jnp.logical_and(there, on), lambda: row_copy(ch, k, to_right, src))
        spread(there, ch, k, src)

    def col_event(ch, k, there):
        relay = jnp.logical_and(there, r // 2 != c // 2)
        partner = {"row": r + 1 - 2 * lax.rem(r, 2)}
        piece = raw.at[1, k, rows(ch)]

        @pl.when(jnp.logical_and(there, jnp.logical_not(hub)))
        def _():
            remote(piece, piece, next_send.at[k], col_recv.at[ch, k], {"row": r}).wait_recv()

        start(jnp.logical_and(relay, lax.rem(r, 2) == lax.rem(k, 2)), lambda: remote(
            piece, piece, relay_send.at[ch, k], col_recv.at[ch, k], partner))

    base = t * nb

    def count(j):
        if j:
            return bars_ref[base + j - 1]
        return jnp.where(t > 0, bars_ref[jnp.maximum(base - 1, 0)], 0)

    def center(j, side):
        b = j - 1 if j else last
        low = down(blk * b)
        depth = up(blk * (b + 1)) - low
        offset = blk * b - low
        first = low if j else spans[before][0]
        n = count(j)
        bar = lax.broadcasted_iota(jnp.int32, (depth, width), 0) - offset
        mask = jnp.logical_and(bar >= 0, bar < n)
        divisor = jnp.full((1, width), jnp.maximum(n, 1).astype(jnp.float32))
        source = 0 if side == 0 else jnp.where(hub, 0, 1)

        def piece(k, carry):
            values = raw[source, k, pl.ds(first, depth), :].astype(jnp.float32)
            mean = jnp.sum(jnp.where(mask, values, 0.0), axis=0, keepdims=True) / divisor
            cent = jnp.where(mask, values - mean, 0.0).astype(jnp.bfloat16)
            wide = cent.astype(jnp.float32)
            stats[side, k, 2 * j : 2 * j + 1, :] = mean
            stats[side, k, 2 * j + 1 : 2 * j + 2, :] = jnp.sum(wide * wide, axis=0, keepdims=True)
            if depth < DEPTH:
                wide = jnp.concatenate([wide, jnp.zeros((DEPTH - depth, width), jnp.float32)], axis=0)
            at = pl.ds(pl.multiple_of(k * width, width), width)
            if side == 0:
                lhs[at, j * DEPTH : (j + 1) * DEPTH] = wide.T.astype(jnp.bfloat16)
            else:
                rhs[j * DEPTH : (j + 1) * DEPTH, at] = wide.astype(jnp.bfloat16)
            return carry

        lax.fori_loop(0, C, piece, 0)

    def weigh(b):
        count_a = jnp.full((1, width), count(b).astype(jnp.float32))
        count_b = jnp.full((1, width), count(b + 1).astype(jnp.float32))
        return count_a * count_b / (count_a + count_b)

    def pair(b, weight, side, k):
        mean_a, var_a = stats[side, k, 2 * b : 2 * b + 1, :], stats[side, k, 2 * b + 1 : 2 * b + 2, :]
        mean_b, var_b = stats[side, k, 2 * b + 2 : 2 * b + 3, :], stats[side, k, 2 * b + 3 : 2 * b + 4, :]
        delta = mean_a - mean_b
        return delta, lax.rsqrt(var_a + var_b + weight * delta * delta)

    def gram_tile(k, j, uses, keep):
        at = slice(k * width, (k + 1) * width)
        sides = []
        for b, other in uses:
            weight = weigh(b)
            delta, inv = pair(b, weight, 0, k)
            both = jnp.concatenate([weight * delta, inv, jnp.zeros((6, width), jnp.float32)], axis=0).T
            sides.append((b, other, weight, both[:, 0:1], both[:, 1:2]))
        a = lhs[at, j * DEPTH : (j + 1) * DEPTH]
        for m in range(R):
            span = slice(m * width, (m + 1) * width)
            gram = jnp.dot(a, rhs[j * DEPTH : (j + 1) * DEPTH, span], preferred_element_type=jnp.float32)
            for b, other, weight, scaled, inv_i in sides:
                delta, inv = pair(b, weight, 1, m)
                cov = gram + other[at, span] + scaled * delta
                out_ref[b, at, span] = (cov * inv_i * inv).astype(jnp.bfloat16)
            if keep is not None:
                keep[at, span] = gram

    order = [last] + list(range(last))
    true = t >= 0
    mine = pltpu.make_async_copy(x_ref, raw.at[0, c, pl.ds(0, nbars)], own_sem)
    bars_copy = pltpu.make_async_copy(bars_in, bars_ref, bars_sem)
    for ch in order[:2]:
        own_send(ch)
        spread(true, ch, c, x_ref.at[rows(ch)])
    mine.start()
    bars_copy.start()

    @pl.when(t == 0)
    def _():
        low, depth = spans[before]
        for side in range(2):
            for k in range(C):
                raw[side, k, pl.ds(low, depth), :] = jnp.zeros((depth, width), jnp.bfloat16)

    events = []
    for i, ch in enumerate(order):
        events.append((ch, c, true, true, None))
        for d in range(1, C):
            events.append((ch, jnp.maximum(c - d, 0), c >= d, c < C - 1, True))
            events.append((ch, jnp.minimum(c + d, C - 1), c + d < C, c > 0, False))
        if i == 1:
            events.extend((before, jnp.int32(k), t > 0, true, None) for k in range(C))

    def ready(j):
        if j == 0:
            needed = {before}
        else:
            low, high = down(blk * (j - 1)), up(blk * j)
            needed = {ch for ch in range(nb) if cuts[ch] < high and cuts[ch + 1] > low}
        return max(e for e, event in enumerate(events) if event[0] in needed)

    tasks = []

    def plan(j, uses, keep):
        for side in range(2):
            tasks.append((ready(j), functools.partial(center, j, side)))
        for k in range(C):
            tasks.append((ready(j), functools.partial(gram_tile, k, j, uses, keep)))

    plan(nb, [], final)
    plan(1, [], kept)
    plan(0, [(0, kept)], None)
    for b in range(1, last):
        uses = [(b, kept)] + ([(last, final)] if b == last - 1 else [])
        plan(b + 1, uses, kept if b < last - 1 else None)

    waited = False
    for e in range(len(events) + LAG):
        if e < len(events):
            row_event(*events[e])
            if e + 1 == len(events) or (events[e + 1][0] != events[e][0]):
                if events[e][0] != before and order.index(events[e][0]) + 2 < nb:
                    ch = order[order.index(events[e][0]) + 2]
                    own_send(ch)
                    spread(true, ch, c, x_ref.at[rows(ch)])
        if e >= LAG:
            col_event(*events[e - LAG][:3])
        if tasks and tasks[0][0] <= e - LAG:
            if not waited:
                mine.wait()
                bars_copy.wait()
                waited = True
            tasks.pop(0)[1]()
    for _, task in tasks:
        task()
    for there, make in sent:

        @pl.when(there)
        def _():
            make().wait_send()


def on_device(sizes, returns, block_bars):
    T, R, C = sizes
    nbars, width = returns.shape
    nb = block_bars.shape[0] // T
    blk = nbars // nb
    tail = nbars - down(blk * (nb - 1))
    dma = pltpu.SemaphoreType.DMA
    return pl.pallas_call(
        functools.partial(kernel, sizes, nb, blk),
        out_shape=pltpu.VMEM((nb, C * width, R * width), jnp.bfloat16),
        in_specs=[pl.BlockSpec(memory_space=pltpu.HBM), pl.BlockSpec(memory_space=pltpu.HBM)],
        out_specs=pl.BlockSpec(memory_space=pltpu.VMEM),
        scratch_shapes=[
            pltpu.SMEM(block_bars.shape, jnp.int32),
            pltpu.VMEM((2, C, nbars + tail, width), jnp.bfloat16),
            pltpu.VMEM((C * width, (nb + 1) * DEPTH), jnp.bfloat16),
            pltpu.VMEM(((nb + 1) * DEPTH, R * width), jnp.bfloat16),
            pltpu.VMEM((2, C, up(2 * (nb + 1)), width), jnp.float32),
            pltpu.VMEM((C * width, R * width), jnp.float32),
            pltpu.VMEM((C * width, R * width), jnp.float32),
            dma,
            dma,
            dma((nb, C, 2)),
            dma((nb + 1, C)),
            dma((C,)),
            dma((nb + 1, C, R // 2)),
            dma((nb + 1, C)),
            dma((nb + 1, C)),
        ],
        compiler_params=pltpu.CompilerParams(
            collective_id=0, has_side_effects=True, vmem_limit_bytes=32 * 1024 * 1024
        ),
        name="gather_correlate",
    )(block_bars, returns)


def solution(mesh):
    sizes = (mesh.shape["tm"], mesh.shape["row"], mesh.shape["col"])
    placed = (P("tm", ("row", "col")), P())
    return jax.shard_map(
        functools.partial(on_device, sizes),
        mesh=mesh, in_specs=placed, out_specs=P("tm", "row", "col"), check_vma=False,
    )
```

time: 63 us -> 58.1 us (0.922)
  Pallas kernels: 57.8 us -> 52.9 us
    pallas_call x1, Pallas kernels: 57.8 us -> 52.9 us  [on_device(): pl.pallas_call(functools.partial(kernel, sizes, nb, blk), out_shape=pltpu...]
where the time goes in v3:
time: 58.1 us; the launch traced here: 57.9 us
  Pallas kernels  52.9 us (91%)
  local copies, waits for them, and re-layouts  5.04 us (9%)
    pallas_call x1, Pallas kernels, on_device(): pl.pallas_call(functools.partial(kernel, sizes, nb, blk), out_shape=pltpu...  52.9 us
    unnamed x5, local copies, waits for them, and re-layouts  5.04 us

profile of v3, /device:TPU:6, one launch (start us, length us, event | category | flops | bytes accessed | tf_op | source)
XLA Modules:
  0.0 57.9 jit_solution(14991898383149970931)
XLA Ops:
  0.0 0.0 copy-start
  0.0 1.0 %copy-done = bf16[720,256]{1,0:T(8,128)(2,1)S(1)} copy-done((bf16[720,256]{1,0:T(8,128)(2,1)S(1)}, bf16[720,256]{1,0:T(8,128)(2,1)}, u32[]{:S(2)}) %copy-start) | copy-done | bytes 368664
  1.0 0.0 copy-start.1
  1.0 0.7 %copy-done.1 = s32[8]{0:T(128)S(1)} copy-done((s32[8]{0:T(128)S(1)}, s32[8]{0:T(128)}, u32[]{:S(2)}) %copy-start.1) | copy-done | bytes 56
  1.6 52.9 %gather_correlate.1 = bf16[4,1024,1024]{2,1,0:T(8,128)(2,1)S(1)} custom-call(s32[8]{0:T(128)S(1)} %copy-done.1, bf16[720,256]{1,0:T(8,128)(2,1)S(1)} %copy-done), custom_call_target="tpu_custom_call" | custom-call | tf_op jit(solution)/shard_map/gather_correlate/pallas_call | solution.py:268
  54.5 3.4 %copy.4 = bf16[4,1024,1024]{2,1,0:T(8,128)(2,1)} copy(bf16[4,1024,1024]{2,1,0:T(8,128)(2,1)S(1)} %gather_correlate.1) | data formatting | bytes 16777216
Async XLA Ops:
  0.0 1.0 %copy-start = (bf16[720,256]{1,0:T(8,128)(2,1)S(1)}, bf16[720,256]{1,0:T(8,128)(2,1)}, u32[]{:S(2)}) copy-start(bf16[720,256]{1,0:T(8,128)(2,1)} %x_ref.1) | copy-start | bytes 1105924
  1.0 0.7 %copy-start.1 = (s32[8]{0:T(128)S(1)}, s32[8]{0:T(128)}, u32[]{:S(2)}) copy-start(s32[8]{0:T(128)} %bars_in.1) | copy-start | bytes 100

commit v4 on v3

v4 whole, which is shorter than its diff:
```python
import functools

import jax
import jax.numpy as jnp
from jax import lax
from jax.experimental import pallas as pl
from jax.experimental.pallas import tpu as pltpu
from jax.sharding import PartitionSpec as P

TILE = 16
DEPTH = 256
MESH = pl.DeviceIdType.MESH


def up(value, step=TILE):
    return -(-value // step) * step


def down(value, step=TILE):
    return value // step * step


def kernel(
    sizes, nb, blk, bars_in, x_ref, out_ref,
    bars_ref, raw, lhs, rhs, row_stats, col_stats, own_sem, bars_sem, row_send, row_recv, next_send, hub_send, col_recv, relay_send,
):
    T, R, C = sizes
    nbars, width = x_ref.shape
    t, r, c = lax.axis_index("tm"), lax.axis_index("row"), lax.axis_index("col")
    hub = r == c
    last = nb - 1
    cuts = [up(blk * b) for b in range(nb - 1)] + [down(blk * last), nbars]
    spans = [(cuts[b], cuts[b + 1] - cuts[b]) for b in range(nb)]
    spans.append((nbars, nbars - cuts[last]))
    before = nb

    def rows(ch):
        return pl.ds(*spans[ch])

    barrier = pltpu.get_barrier_semaphore()

    def greet(where):
        pl.semaphore_signal(barrier, inc=1, device_id=where, device_id_type=MESH)

    ends = ((c > 0, {"col": c - 1}), (c < C - 1, {"col": c + 1}), (t > 0, {"tm": t - 1}), (t < T - 1, {"tm": t + 1}))
    expected = R - 1
    for there, where in ends:
        pl.when(there)(functools.partial(greet, where))
        expected = expected + there.astype(jnp.int32)
    for step in range(1, R):
        greet({"row": lax.rem(r + step, R)})
    pl.semaphore_wait(barrier, expected)

    def remote(src, dst, send, recv, where):
        return pltpu.make_async_remote_copy(
            src_ref=src, dst_ref=dst, send_sem=send, recv_sem=recv, device_id=where, device_id_type=MESH
        )

    sent = []

    def start(there, make):
        @pl.when(there)
        def _():
            make().start()

        sent.append((there, make))

    def row_copy(ch, k, to_right, src):
        where = {"col": c + 1 if to_right else c - 1}
        return remote(src, raw.at[0, k, rows(ch)], row_send.at[ch, k, int(to_right)], row_recv.at[ch, k], where)

    def own_send(ch):
        src = x_ref.at[rows(ch)]
        start(c < C - 1, lambda: row_copy(ch, c, True, src))
        start(c > 0, lambda: row_copy(ch, c, False, src))

    def spread(there, ch, k, src):
        at_hub = jnp.logical_and(there, hub)
        chips = R // 2
        chip = r // 2
        for step in range(1, chips):
            where = {"row": 2 * lax.rem(chip + step, chips) + lax.rem(k, 2)}
            start(at_hub, lambda where=where, step=step: remote(
                src, raw.at[1, k, rows(ch)], hub_send.at[ch, k, step], col_recv.at[ch, k], where))
        partner = {"row": r + 1 - 2 * lax.rem(r, 2)}
        start(at_hub, lambda: remote(src, raw.at[1, k, rows(ch)], hub_send.at[ch, k, 0], col_recv.at[ch, k], partner))
        if ch == last:
            start(jnp.logical_and(there, t < T - 1), lambda: remote(
                src, raw.at[0, k, rows(before)], next_send.at[k], row_recv.at[before, k], {"tm": t + 1}))

    def row_arrive(there, ch, k):
        @pl.when(there)
        def _():
            piece = raw.at[0, k, rows(ch)]
            remote(piece, piece, next_send.at[k], row_recv.at[ch, k], {"row": r}).wait_recv()

    def row_event(ch, k, there, on, to_right):
        if to_right is None and ch != before:
            return
        row_arrive(there, ch, k)
        src = raw.at[0, k, rows(ch)]
        if ch != before:
            start(jnp.logical_and(there, on), lambda: row_copy(ch, k, to_right, src))
        spread(there, ch, k, src)

    def col_event(ch, k, there):
        relay = jnp.logical_and(there, r // 2 != c // 2)
        partner = {"row": r + 1 - 2 * lax.rem(r, 2)}
        piece = raw.at[1, k, rows(ch)]

        @pl.when(jnp.logical_and(there, jnp.logical_not(hub)))
        def _():
            remote(piece, piece, next_send.at[k], col_recv.at[ch, k], {"row": r}).wait_recv()

        start(jnp.logical_and(relay, lax.rem(r, 2) == lax.rem(k, 2)), lambda: remote(
            piece, piece, relay_send.at[ch, k], col_recv.at[ch, k], partner))

    base = t * nb

    def count(j):
        if j:
            return bars_ref[base + j - 1]
        return jnp.where(t > 0, bars_ref[jnp.maximum(base - 1, 0)], 0)

    def moments(j, n, values):
        b = j - 1 if j else last
        low = down(blk * b)
        depth = up(blk * (b + 1)) - low
        offset = blk * b - low
        first = low if j else spans[before][0]
        bar = lax.broadcasted_iota(jnp.int32, (depth, width), 0) - offset
        mask = jnp.logical_and(bar >= 0, bar < n)
        values = values(first, depth).astype(jnp.float32)
        divisor = jnp.full((1, width), jnp.maximum(n, 1).astype(jnp.float32))
        mean = jnp.sum(jnp.where(mask, values, 0.0), axis=0, keepdims=True) / divisor
        wide = jnp.where(mask, values - mean, 0.0).astype(jnp.bfloat16).astype(jnp.float32)
        var = jnp.sum(wide * wide, axis=0, keepdims=True)
        if depth < DEPTH:
            wide = jnp.concatenate([wide, jnp.zeros((DEPTH - depth, width), jnp.float32)], axis=0)
        return mean, var, wide

    def center(k):
        at = pl.ds(pl.multiple_of(k * width, width), width)
        counts = [count(j) for j in range(nb + 1)]
        for side in range(2):
            source = 0 if side == 0 else jnp.where(hub, 0, 1)
            means, variances = [], []
            for j in range(nb + 1):
                mean, var, wide = moments(j, counts[j], lambda first, depth: raw[source, k, pl.ds(first, depth), :])
                means.append(mean)
                variances.append(var)
                if side == 0:
                    lhs[at, j * DEPTH : (j + 1) * DEPTH] = wide.T.astype(jnp.bfloat16)
                else:
                    rhs[j * DEPTH : (j + 1) * DEPTH, at] = wide.astype(jnp.bfloat16)
            lines = []
            for b in range(nb):
                count_a = jnp.full((1, width), counts[b].astype(jnp.float32))
                count_b = jnp.full((1, width), counts[b + 1].astype(jnp.float32))
                weight = count_a * count_b / (count_a + count_b)
                delta = means[b] - means[b + 1]
                inv = lax.rsqrt(variances[b] + variances[b + 1] + weight * delta * delta)
                lines.extend([weight * delta if side == 0 else delta, inv])
            spare = up(2 * nb, 8) - 2 * nb
            if spare:
                lines.append(jnp.zeros((spare, width), jnp.float32))
            lines = jnp.concatenate(lines, axis=0)
            if side == 0:
                row_stats[k] = lines.T
            else:
                col_stats[k] = lines

    def tile(kr, kc):
        down_at = pl.ds(pl.multiple_of(kr * width, width), width)
        over_at = pl.ds(pl.multiple_of(kc * width, width), width)
        previous = None
        for j in range(nb + 1):
            span = slice(j * DEPTH, (j + 1) * DEPTH)
            gram = jnp.dot(lhs[down_at, span], rhs[span, over_at], preferred_element_type=jnp.float32)
            if j:
                b = j - 1
                scaled, inv_i = row_stats[kr, :, 2 * b : 2 * b + 1], row_stats[kr, :, 2 * b + 1 : 2 * b + 2]
                delta, inv = col_stats[kc, 2 * b : 2 * b + 1, :], col_stats[kc, 2 * b + 1 : 2 * b + 2, :]
                cov = previous + gram + scaled * delta
                out_ref[b, down_at, over_at] = (cov * inv_i * inv).astype(jnp.bfloat16)
            previous = gram

    near = jnp.minimum(c, C - 1 - c)

    def source_at(p):
        both = jnp.where(lax.rem(p, 2) == 1, c - (p + 1) // 2, c + p // 2)
        one = jnp.where(2 * c < C - 1, c + p - near, c - p + near)
        return jnp.where(p <= 2 * near, both, one)

    def within(d):
        return jnp.minimum(c, d) + jnp.minimum(C - 1 - c, d) + 1

    def compute(d):
        def shell(p, carry):
            k = source_at(p)
            center(k)

            def one(n, carry):
                other = source_at(jnp.where(n <= p, n, n - p - 1))
                tile(jnp.where(n <= p, k, other), jnp.where(n <= p, other, k))
                return carry

            return lax.fori_loop(0, 2 * p + 1, one, carry)

        lax.fori_loop(within(d - 1) if d else 0, within(d), shell, 0)

    order = [last] + list(range(last))
    true = t >= 0
    mine = pltpu.make_async_copy(x_ref, raw.at[0, c, pl.ds(0, nbars)], own_sem)
    bars_copy = pltpu.make_async_copy(bars_in, bars_ref, bars_sem)
    for ch in order:
        own_send(ch)
        spread(true, ch, c, x_ref.at[rows(ch)])
    mine.start()
    bars_copy.start()

    @pl.when(t == 0)
    def _():
        low, depth = spans[before]
        for side in range(2):
            for k in range(C):
                raw[side, k, pl.ds(low, depth), :] = jnp.zeros((depth, width), jnp.bfloat16)

    def at_distance(d):
        if d == 0:
            return [(c, true, True)]
        return [(jnp.maximum(c - d, 0), c >= d, True), (jnp.minimum(c + d, C - 1), c + d < C, False)]

    def row_events(ch, d):
        for k, there, to_right in at_distance(d):
            if ch == before:
                row_event(ch, k, jnp.logical_and(there, t > 0), true, None)
            else:
                row_event(ch, k, there, c < C - 1 if to_right else c > 0, to_right)

    def col_events(ch, d):
        for k, there, _ in at_distance(d):
            col_event(ch, k, jnp.logical_and(there, t > 0) if ch == before else there)

    for d in range(1, C + 1):
        for i, ch in enumerate(order):
            if d < C:
                row_events(ch, d)
            if i == 0:
                row_events(before, d - 1)
                for other in order:
                    col_events(other, d - 1)
            if i == 1:
                col_events(before, d - 1)
                if d == 1:
                    mine.wait()
                    bars_copy.wait()
                compute(d - 1)
    for there, make in sent:

        @pl.when(there)
        def _():
            make().wait_send()


def on_device(sizes, returns, block_bars):
    T, R, C = sizes
    nbars, width = returns.shape
    nb = block_bars.shape[0] // T
    blk = nbars // nb
    tail = nbars - down(blk * (nb - 1))
    dma = pltpu.SemaphoreType.DMA
    return pl.pallas_call(
        functools.partial(kernel, sizes, nb, blk),
        out_shape=pltpu.VMEM((nb, C * width, R * width), jnp.bfloat16),
        in_specs=[pl.BlockSpec(memory_space=pltpu.HBM), pl.BlockSpec(memory_space=pltpu.HBM)],
        out_specs=pl.BlockSpec(memory_space=pltpu.VMEM),
        scratch_shapes=[
            pltpu.SMEM(block_bars.shape, jnp.int32),
            pltpu.VMEM((2, C, nbars + tail, width), jnp.bfloat16),
            pltpu.VMEM((C * width, (nb + 1) * DEPTH), jnp.bfloat16),
            pltpu.VMEM(((nb + 1) * DEPTH, R * width), jnp.bfloat16),
            pltpu.VMEM((C, width, up(2 * nb, 8)), jnp.float32),
            pltpu.VMEM((C, up(2 * nb, 8), width), jnp.float32),
            dma,
            dma,
            dma((nb, C, 2)),
            dma((nb + 1, C)),
            dma((C,)),
            dma((nb + 1, C, R // 2)),
            dma((nb + 1, C)),
            dma((nb + 1, C)),
        ],
        compiler_params=pltpu.CompilerParams(
            collective_id=0, has_side_effects=True, vmem_limit_bytes=58650624
        ),
        name="gather_correlate",
    )(block_bars, returns)


def solution(mesh):
    sizes = (mesh.shape["tm"], mesh.shape["row"], mesh.shape["col"])
    placed = (P("tm", ("row", "col")), P())
    return jax.shard_map(
        functools.partial(on_device, sizes),
        mesh=mesh, in_specs=placed, out_specs=P("tm", "row", "col"), check_vma=False,
    )
```

time: 58.1 us -> 42.7 us (0.73)
  Pallas kernels: 52.9 us -> 39.2 us
  local copies, waits for them, and re-layouts: 5.04 us -> 3.4 us
    pallas_call x1, Pallas kernels: 52.9 us -> 39.2 us  [on_device(): pl.pallas_call(functools.partial(kernel, sizes, nb, blk), out_shape=pltpu...]
    unnamed x5 -> x1, local copies, waits for them, and re-layouts: 5.04 us -> 3.4 us
where the time goes in v4:
time: 42.7 us; the launch traced here: 42.6 us
  Pallas kernels  39.2 us (92%)
  local copies, waits for them, and re-layouts  3.4 us (8%)
    pallas_call x1, Pallas kernels, on_device(): pl.pallas_call(functools.partial(kernel, sizes, nb, blk), out_shape=pltpu...  39.2 us
    unnamed x1, local copies, waits for them, and re-layouts  3.4 us

profile of v4, /device:TPU:6, one launch (start us, length us, event | category | flops | bytes accessed | tf_op | source)
XLA Modules:
  0.0 42.6 jit_solution(17119018847127790098)
XLA Ops:
  0.0 39.2 %gather_correlate.1 = bf16[4,1024,1024]{2,1,0:T(8,128)(2,1)S(1)} custom-call(s32[8]{0:T(128)} %bars_in.1, bf16[720,256]{1,0:T(8,128)(2,1)} %x_ref.1), custom_call_target="tpu_custom_call" | custom-call | tf_op jit(solution)/shard_map/gather_correlate/pallas_call | solution.py:273
  39.2 3.4 %copy.4 = bf16[4,1024,1024]{2,1,0:T(8,128)(2,1)} copy(bf16[4,1024,1024]{2,1,0:T(8,128)(2,1)S(1)} %gather_correlate.1) | data formatting | bytes 16777216
